TPU v7x, 32 devices: a whole 2x2x4 slice. The times are simulated.
32 devices in a mesh: seq: 16 (over z, y, core), head: 2 (over x).
Axes of the slice: x: 2, y: 2, z: 4, core: 2. Of those that a mesh axis runs over, the one named last changes fastest.
Arguments:
- tokens: bfloat16 [512, 2048], P('seq', 'head'), may hold values from -6 to 6
- ln1_gain: float32 [2048], replicated, may hold values from 0.1 to 1.9
- ln1_shift: float32 [2048], replicated, may hold values from -1.75 to 1.75
- ln2_gain: float32 [2048], replicated, may hold values from 0.1 to 1.9
- ln2_shift: float32 [2048], replicated, may hold values from -1.75 to 1.75
- w_qkv: bfloat16 [2048, 3, 2048], P(None, None, 'head'), may hold values from -0.125 to 0.125
- b_qkv: float32 [3, 2048], P(None, 'head'), may hold values from -3 to 3
- w_dense: bfloat16 [2048, 2048], P('head'), may hold values from -0.125 to 0.125
- b_dense: float32 [2048], P('head'), may hold values from -1.75 to 1.75
- w_up: bfloat16 [2048, 4096], P(None, 'head'), may hold values from -0.125 to 0.125
- b_up: float32 [4096], P('head'), may hold values from -3 to 3
- w_down: bfloat16 [4096, 2048], P('head'), may hold values from -0.09375 to 0.09375
- b_down: float32 [2048], P('head'), may hold values from -1.75 to 1.75
- keys_short: bfloat16 [512, 64, 2048], P('seq', None, 'head'), may hold values from -210 to 210
- values_short: bfloat16 [512, 64, 2048], P('seq', None, 'head'), may hold values from -16 to 16
- keys_long: bfloat16 [32768, 2048], P('seq', 'head'), may hold values from -210 to 210
- values_long: bfloat16 [32768, 2048], P('seq', 'head'), may hold values from -16 to 16
- lengths: int32 [512], replicated, may hold values from 16 to 8192, as said below
- slot_request: int32 [512], replicated, may hold values from 0 to 511, as said below
- piece_map: int32 [16], replicated, may hold values from 0 to 15, each once
Outputs:
- layer_out: bfloat16 [512, 2048], P('seq', 'head')
Inputs may be any that keep to these rules, and one draw needn't show every extreme that they name: `lengths`: requests 0 to 3 hold more than 4096 positions, one of them exactly 8192; every other request holds 16 to 64 positions, one of them exactly 64. `slot_request`: A permutation of the requests; slot s lies on index s // 32 of seq. The requests 32 h to 32 h + 31 are served in 8 groups of exactly 4 on as many different indices of seq. Rows 2048 b to 2048 b + 2047 of keys_long and values_long hold positions (piece_map[b] % 4) * 2048 onwards of the cache of request piece_map[b] // 4.
All inputs are finite; a program needn't handle non-finite values.
Results may differ from a plain program's by a relative error of at most 0.0095.
Values may be sent and summed in bfloat16 or wider, within the bound.
A program may use at most 192 MiB of HBM per device.

v0:
```python
import jax
import jax.numpy as jnp
from jax import lax
from jax.sharding import PartitionSpec as P

HD = 256
ROT = 64
LONGS = 4
epsilon = 1e-05
very_low = -1e30


def merged(array, axis, combine):
    everything = jax.tree.map(lambda part: lax.all_gather(part, axis), array)
    first = jax.tree.map(lambda part: part[0], everything)

    def hop(k, so_far):
        return combine(so_far, jax.tree.map(lambda part: part[k], everything))

    return lax.fori_loop(1, lax.axis_size(axis), hop, first)


def layer_norm(values, gain, shift):
    center = jnp.mean(values, axis=-1, keepdims=True)
    offset = values - center
    spread = jnp.mean(offset * offset, axis=-1, keepdims=True)
    return offset * lax.rsqrt(spread + epsilon) * gain + shift


def rotary(values, position):
    half_rot = ROT // 2
    frequency = jnp.power(10000.0, -2.0 * jnp.arange(half_rot, dtype=jnp.float32) / ROT)
    angles = position.astype(jnp.float32)[:, None] * frequency[None, :]
    cosine = jnp.cos(angles)[:, None, :]
    sine_of = jnp.sin(angles)[:, None, :]
    leading = values[..., :half_rot]
    trailing = values[..., half_rot:ROT]
    return jnp.concatenate(
        [
            leading * cosine - trailing * sine_of,
            trailing * cosine + leading * sine_of,
            values[..., ROT:],
        ],
        axis=-1,
    )


def attend(queries, key_rows, value_rows, usable):
    scores = jnp.einsum(
        "rhc,rthc->rht", queries, key_rows, preferred_element_type=jnp.float32
    ) * HD ** (-0.5)
    masked = jnp.where(usable[:, None, :], scores, very_low)
    summit = jnp.max(masked, axis=-1)
    weights = jnp.where(usable[:, None, :], jnp.exp(masked - summit[..., None]), 0.0)
    amount = jnp.sum(weights, axis=-1)
    mixed = jnp.einsum(
        "rht,rthc->rhc",
        weights.astype(jnp.bfloat16),
        value_rows,
        preferred_element_type=jnp.float32,
    )
    return (summit, amount, mixed)


def combine_partials(first_part, second_part):
    top_first, total_first, out_first = first_part
    top_second, total_second, out_second = second_part
    summit = jnp.maximum(top_first, top_second)
    scale_first = jnp.exp(top_first - summit)
    scale_second = jnp.exp(top_second - summit)
    total_both = total_first * scale_first + total_second * scale_second
    out_both = out_first * scale_first[..., None] + out_second * scale_second[..., None]
    return (summit, total_both, out_both)


def local(
    tokens,
    ln1_gain,
    ln1_shift,
    ln2_gain,
    ln2_shift,
    w_qkv,
    b_qkv,
    w_dense,
    b_dense,
    w_up,
    b_up,
    w_down,
    b_down,
    keys_short,
    values_short,
    keys_long,
    values_long,
    lengths,
    slot_request,
    piece_map,
):
    slot_rows, part_width = tokens.shape
    seq_count = lax.axis_size("seq")
    seq_place = lax.axis_index("seq")
    request_count = slot_request.shape[0]
    heads_here = part_width // HD
    my_requests = lax.dynamic_slice_in_dim(slot_request, seq_place * slot_rows, slot_rows)
    shard_rows = lax.all_gather(tokens, "seq", axis=0, tiled=True)
    row_ids = jnp.arange(shard_rows.shape[0], dtype=jnp.int32)
    selector = (my_requests[:, None] == row_ids[None, :]).astype(jnp.bfloat16)
    own_cols = jnp.dot(selector, shard_rows, preferred_element_type=jnp.float32).astype(
        jnp.bfloat16
    )
    full_rows = lax.all_gather(own_cols, "head", axis=1, tiled=True)
    resident = full_rows.astype(jnp.float32)
    normed_attn = layer_norm(resident, ln1_gain, ln1_shift).astype(jnp.bfloat16)
    normed_mlp = layer_norm(resident, ln2_gain, ln2_shift).astype(jnp.bfloat16)
    projected = jnp.dot(
        normed_attn,
        w_qkv.reshape(w_qkv.shape[0], 3 * part_width),
        preferred_element_type=jnp.float32,
    )
    projected = projected.reshape(slot_rows, 3, part_width) + b_qkv[None]
    request_ids = jnp.arange(request_count, dtype=jnp.int32)
    my_lengths = jnp.sum(
        jnp.where(my_requests[:, None] == request_ids[None, :], lengths[None, :], 0), axis=1
    )
    queries = rotary(projected[:, 0].reshape(slot_rows, heads_here, HD), my_lengths).astype(
        jnp.bfloat16
    )
    new_keys = rotary(projected[:, 1].reshape(slot_rows, heads_here, HD), my_lengths).astype(
        jnp.bfloat16
    )
    new_values = projected[:, 2].reshape(slot_rows, heads_here, HD).astype(jnp.bfloat16)
    long_hits = my_requests[:, None] == jnp.arange(LONGS, dtype=jnp.int32)[None, :]
    long_part = jnp.sum(
        jnp.where(long_hits[:, :, None, None], queries.astype(jnp.float32)[:, None], 0.0), axis=0
    )
    long_queries = lax.psum(long_part, "seq")
    short_max = keys_short.shape[1]
    short_usable = (jnp.arange(short_max, dtype=jnp.int32)[None, :] < my_lengths[:, None]) & (
        my_lengths <= short_max
    )[:, None]
    short_keys = keys_short.reshape(slot_rows, short_max, heads_here, HD)
    short_vals = values_short.reshape(slot_rows, short_max, heads_here, HD)
    short_top, short_total, short_out = attend(queries, short_keys, short_vals, short_usable)
    own_score = jnp.sum(
        queries.astype(jnp.float32) * new_keys.astype(jnp.float32), axis=-1
    ) * HD ** (-0.5)
    piece_count = seq_count // LONGS
    my_piece = lax.dynamic_slice_in_dim(piece_map, seq_place, 1)[0]
    long_owner = my_piece // piece_count
    piece_index = my_piece % piece_count
    long_pick = jnp.arange(LONGS, dtype=jnp.int32) == long_owner
    piece_query = jnp.sum(jnp.where(long_pick[:, None, None], long_queries, 0.0), axis=0).astype(
        jnp.bfloat16
    )
    long_length = jnp.sum(jnp.where(long_pick, lengths[:LONGS], 0))
    piece_len = keys_long.shape[0]
    positions = piece_index * piece_len + jnp.arange(piece_len, dtype=jnp.int32)
    piece_usable = (positions < long_length)[None, :]
    piece_keys = keys_long.reshape(1, piece_len, heads_here, HD)
    piece_vals = values_long.reshape(1, piece_len, heads_here, HD)
    piece_top, piece_total, piece_out = attend(
        piece_query[None], piece_keys, piece_vals, piece_usable
    )
    spread_top = jnp.where(long_pick[:, None], piece_top, very_low)
    spread_total = jnp.where(long_pick[:, None], piece_total, 0.0)
    spread_out = jnp.where(long_pick[:, None, None], piece_out, 0.0)
    long_top, long_total, long_out = merged(
        (spread_top, spread_total, spread_out), "seq", combine_partials
    )
    has_long = jnp.any(long_hits, axis=1)
    mine_top = jnp.where(
        has_long[:, None],
        jnp.sum(jnp.where(long_hits[:, :, None], long_top[None], 0.0), axis=1),
        very_low,
    )
    mine_total = jnp.sum(jnp.where(long_hits[:, :, None], long_total[None], 0.0), axis=1)
    mine_out = jnp.sum(jnp.where(long_hits[:, :, None, None], long_out[None], 0.0), axis=1)
    summit = jnp.maximum(jnp.maximum(short_top, own_score), mine_top)
    short_scale = jnp.exp(short_top - summit)
    own_scale = jnp.exp(own_score - summit)
    long_scale = jnp.exp(mine_top - summit)
    denominator = short_total * short_scale + own_scale + mine_total * long_scale
    numerator = (
        short_out * short_scale[..., None]
        + new_values.astype(jnp.float32) * own_scale[..., None]
        + mine_out * long_scale[..., None]
    )
    attended = (
        (numerator / denominator[..., None]).reshape(slot_rows, part_width).astype(jnp.bfloat16)
    )
    hidden_units = jax.nn.gelu(
        jnp.dot(normed_mlp, w_up, preferred_element_type=jnp.float32) + b_up, approximate=False
    ).astype(jnp.bfloat16)
    partial_sum = jnp.dot(attended, w_dense, preferred_element_type=jnp.float32) + jnp.dot(
        hidden_units, w_down, preferred_element_type=jnp.float32
    )
    head_total = lax.psum_scatter(
        partial_sum.astype(jnp.bfloat16), "head", scatter_dimension=1, tiled=True
    ).astype(jnp.float32)
    finished = (own_cols.astype(jnp.float32) + head_total + b_dense + b_down).astype(jnp.bfloat16)
    home_ids = seq_place * slot_rows + jnp.arange(slot_rows, dtype=jnp.int32)
    selector = (slot_request[None, :] == home_ids[:, None]).astype(jnp.bfloat16)
    return jnp.dot(
        selector,
        lax.all_gather(finished, "seq", axis=0, tiled=True),
        preferred_element_type=jnp.float32,
    ).astype(jnp.bfloat16)


def solution(mesh):
    in_specs = (
        P("seq", "head"),
        P(),
        P(),
        P(),
        P(),
        P(None, None, "head"),
        P(None, "head"),
        P("head", None),
        P("head"),
        P(None, "head"),
        P("head"),
        P("head", None),
        P("head"),
        P("seq", None, "head"),
        P("seq", None, "head"),
        P("seq", "head"),
        P("seq", "head"),
        P(),
        P(),
        P(),
    )
    out_specs = P("seq", "head")
    return jax.shard_map(local, mesh=mesh, in_specs=in_specs, out_specs=out_specs, check_vma=False)
```

profile of v0, /device:TPU:0, one launch (start us, length us, event | category | flops | bytes accessed | tf_op | source)
XLA Modules:
  0.0 262.1 jit_solution(12537288334544157710)
XLA Ops:
  6.5 0.7 all-gather.3.cloned.1.call-update
  7.3 1.2 dynamic_slice.37
  11.2 17.0 %copy.30 = bf16[2048,3,1024]{0,2,1:T(8,128)(2,1)} copy(bf16[2048,3,1024]{2,0,1:T(8,128)(2,1)} %param.27) | data formatting | bytes 25165824 | tf_op args[5]
  28.5 6.5 %copy.47 = bf16[2048,1024]{0,1:T(8,128)(2,1)} copy(bf16[2048,1024]{1,0:T(8,128)(2,1)} %param.37) | data formatting | bytes 8388608 | tf_op jit(solution)/shard_map/reshape.2
  35.0 0.6 select_reduce_fusion.6
  36.5 13.8 %all-gather.3.cloned.1.call-done = bf16[512,1024]{1,0:T(8,128)(2,1)} async-done(((bf16[32,1024]{1,0:T(8,128)(2,1)}), bf16[512,1024]{1,0:T(8,128)(2,1)}) %all-gather.3.cloned.1.call-update) | async-done | bytes 1048592 | tf_op jit(solution)/shard_map/all_gather | solution.py:104
  50.3 1.5 convolution_convert_fusion.1
  51.8 4.9 %all_gather.22 = bf16[32,2048]{1,0:T(8,128)(2,1)S(1)} all-gather(bf16[32,1024]{1,0:T(8,128)(2,1)S(1)} %convolution_convert_fusion.1), channel_id=1, replica_groups=mesh['seq'=16,'head'=2] {'head'}, dimensions={1}, use_global_device_ids=true | all-gather | bytes 196608 | tf_op jit(solution)/shard_map/all_gather | solution.py:110
  57.2 8.5 %fusion.15 = f32[32,3,1024]{2,0,1:T(8,128)S(1)} fusion(bf16[2048,3,1024]{0,2,1:T(8,128)(2,1)} %copy.30, f32[3,1024]{1,0:T(4,128)S(1)} %copy-done.1, bf16[32,2048]{1,0:T(8,128)(2,1)S(1)} %all_gather.22, f32[2048]{0:T(1024)S(1)} %copy-done.5, f32[2048]{0:T(1024)S(1)} %copy-done.6, f32[32]{0:T(128)S(1)} %add_rsqrt_fusion, f32[32]{0:T(128)S(1)} %broadcast_multiply_fusion), kind=kOutput, calls=%fused_computation.22 | convolution fusion | flops 403144704 | bytes 13136128 | tf_op jit(solution)/shard_map/dot_general | solution.py:114
  66.6 3.4 %fusion.11 = f32[32,4,1,64]{3,2,1,0:T(1,128)S(1)} fusion(bf16[32,8,4,8,256]{4,3,2,1,0:T(8,128)(2,1)} %bitcast.118, bf16[32,4,256,1]{2,1,0,3:T(4,128)(2,1)S(1)} %bitcast.115), kind=kOutput, calls=%fused_computation.16 | convolution fusion | flops 4194304 | bytes 4292608 | tf_op jit(solution)/shard_map/rhc,rthc->rht/dot_general | solution.py:49
  70.4 58.4 %psum.7 = f32[4,4,256]{2,1,0:T(4,128)S(1)} all-reduce(f32[4,4,256]{2,1,0:T(4,128)S(1)} %select_reduce_fusion.1), channel_id=1, replica_groups=mesh['seq'=16,'head'=2] {'seq'}, use_global_device_ids=true, to_apply=%region_8.9 | all-reduce | flops 4096 | bytes 32768 | tf_op jit(solution)/shard_map/psum | solution.py:135
  128.9 3.0 %fusion.108 = f32[4,1,2048]{2,1,0:T(1,128)S(1)} fusion(bf16[2048,4,256]{0,2,1:T(8,128)(2,1)} %bitcast.112, bf16[4,256,1]{1,0,2:T(4,128)(2,1)S(1)} %bitcast.116), kind=kOutput, calls=%fused_computation.149 | convolution fusion | flops 4194304 | bytes 4229120 | tf_op jit(solution)/shard_map/rhc,rthc->rht/dot_general | solution.py:49
  132.3 0.7 fusion.5
  133.0 17.8 %all_gather.25 = f32[16,4,4,256]{3,2,1,0:T(4,128)S(1)} all-gather(f32[1,4,4,256]{3,2,1,0:T(4,128)S(1)} %broadcast_select_fusion), channel_id=1, replica_groups=mesh['seq'=16,'head'=2] {'seq'}, dimensions={0}, use_global_device_ids=true | all-gather | bytes 278528 | tf_op jit(solution)/shard_map/all_gather | solution.py:14
  150.9 19.3 %all_gather.24 = f32[16,4,4]{2,1,0:T(4,128)S(1)} all-gather(f32[1,4,4]{2,1,0:T(4,128)S(1)} %get-tuple-element.228), channel_id=1, replica_groups=mesh['seq'=16,'head'=2] {'seq'}, dimensions={0}, use_global_device_ids=true | all-gather | bytes 1088 | tf_op jit(solution)/shard_map/all_gather | solution.py:14
  170.2 17.7 %all_gather.23 = f32[16,4,4]{2,1,0:T(4,128)S(1)} all-gather(f32[1,4,4]{2,1,0:T(4,128)S(1)} %get-tuple-element.229), channel_id=1, replica_groups=mesh['seq'=16,'head'=2] {'seq'}, dimensions={0}, use_global_device_ids=true | all-gather | bytes 1088 | tf_op jit(solution)/shard_map/all_gather | solution.py:14
  187.9 2.0 while.19
  190.1 3.0 %fusion.8 = f32[32,4,1,256]{3,2,1,0:T(1,128)S(1)} fusion(bf16[32,8,4,8,256]{4,3,2,1,0:T(8,128)(2,1)} %bitcast.113, bf16[32,4,64,1]{2,0,1,3:T(8,128)(2,1)S(1)} %get-tuple-element.218), kind=kOutput, calls=%fused_computation.13 | convolution fusion | flops 4194304 | bytes 4341760 | tf_op jit(solution)/shard_map/rht,rthc->rhc/dot_general | solution.py:56
  193.5 0.8 fusion.143
  194.4 10.0 %fusion.14 = bf16[32,2048]{1,0:T(8,128)(2,1)} fusion(f32[32,2048]{1,0:T(8,128)S(1)} %fusion.143, bf16[2048,2048]{1,0:T(8,128)(2,1)} %param.33, bf16[2048,2048]{1,0:T(8,128)(2,1)} %param.31, bf16[32,2048]{1,0:T(8,128)(2,1)S(1)} %all_gather.22, f32[2048]{0:T(1024)S(1)} %copy-done.2, f32[2048]{0:T(1024)S(1)} %copy-done.3, f32[2048]{0:T(1024)S(1)} %copy-done.4, ...), kind=kOutput, calls=%fused_computation.21 | convolution fusion | flops 541720576 | bytes 17326336 | tf_op jit(solution)/shard_map/dot_general | solution.py:193
  204.5 8.8 %reduce-scatter.2.cloned.1.call-done = bf16[32,1024]{1,0:T(8,128)(2,1)} async-done(((bf16[32,2048]{1,0:T(8,128)(2,1)}), bf16[32,1024]{1,0:T(8,128)(2,1)}) %reduce-scatter.2.cloned.1.call-update) | async-done | bytes 65552 | tf_op jit(solution)/shard_map/reduce_scatter | solution.py:196
  213.2 1.5 add_convert_fusion
  214.8 38.6 %all-gather.5.cloned.1.call-done = bf16[512,1024]{1,0:T(8,128)(2,1)} async-done(((bf16[32,1024]{1,0:T(8,128)(2,1)}), bf16[512,1024]{1,0:T(8,128)(2,1)}) %all-gather.5.cloned.1.call-update) | async-done | bytes 1048592 | tf_op jit(solution)/shard_map/all_gather | solution.py:204
  253.4 2.2 convolution_convert_fusion
  (102 shorter events, 5.9 us)
Async XLA Ops:
  6.5 43.8 %all-gather.3.cloned.1.call-start = ((), (), s32[]{:S(2)}) async-start(), calls=%async_computation.1 | async-start | bytes 1114112 | tf_op jit(solution)/shard_map/all_gather | solution.py:104
  7.3 206.0 %reduce-scatter.2.cloned.1.call-start = ((), (), s32[]{:S(2)}) async-start(), calls=%async_computation.2 | async-start | bytes 196608 | tf_op jit(solution)/shard_map/reduce_scatter | solution.py:196
  11.2 17.0 %copy-start.9 = (s32[512]{0:T(512)S(1)}, s32[512]{0:T(512)}, u32[]{:S(2)}) copy-start(s32[512]{0:T(512)} %param.40) | copy-start | bytes 6148
  11.2 17.1 %copy-start.10 = (s32[512]{0:T(512)S(1)}, s32[512]{0:T(512)}, u32[]{:S(2)}) copy-start(s32[512]{0:T(512)} %param.39) | copy-start | bytes 6148
  28.4 28.7 %copy-start.1 = (f32[3,1024]{1,0:T(4,128)S(1)}, f32[3,1024]{1,0:T(4,128)}, u32[]{:S(2)}) copy-start(f32[3,1024]{1,0:T(4,128)} %param.28) | copy-start | bytes 36868
  28.4 28.7 %copy-start.5 = (f32[2048]{0:T(1024)S(1)}, f32[2048]{0:T(1024)}, u32[]{:S(2)}) copy-start(f32[2048]{0:T(1024)} %param.24) | copy-start | bytes 24580
  28.5 28.7 %copy-start.6 = (f32[2048]{0:T(1024)S(1)}, f32[2048]{0:T(1024)}, u32[]{:S(2)}) copy-start(f32[2048]{0:T(1024)} %param.23) | copy-start | bytes 24580
  128.8 3.4 %copy-start.11 = (bf16[2048,1024]{1,0:T(8,128)(2,1)S(1)}, bf16[2048,1024]{1,0:T(8,128)(2,1)}, u32[]{:S(2)}) copy-start(bf16[2048,1024]{1,0:T(8,128)(2,1)} %param.38) | copy-start | bytes 12582916
  190.1 3.5 %copy-start = (bf16[1024,2048]{1,0:T(8,128)(2,1)S(1)}, bf16[1024,2048]{1,0:T(8,128)(2,1)}, u32[]{:S(2)}) copy-start(bf16[1024,2048]{1,0:T(8,128)(2,1)} %param.29) | copy-start | bytes 12582916
  190.1 4.3 %copy-start.2 = (f32[2048]{0:T(1024)S(1)}, f32[2048]{0:T(1024)}, u32[]{:S(2)}) copy-start(f32[2048]{0:T(1024)} %param.32) | copy-start | bytes 24580
  190.1 4.3 %copy-start.3 = (f32[2048]{0:T(1024)S(1)}, f32[2048]{0:T(1024)}, u32[]{:S(2)}) copy-start(f32[2048]{0:T(1024)} %param.26) | copy-start | bytes 24580
  190.1 4.3 %copy-start.4 = (f32[2048]{0:T(1024)S(1)}, f32[2048]{0:T(1024)}, u32[]{:S(2)}) copy-start(f32[2048]{0:T(1024)} %param.25) | copy-start | bytes 24580
  194.4 18.9 %copy-start.7 = (f32[1024]{0:T(1024)S(1)}, f32[1024]{0:T(1024)}, u32[]{:S(2)}) copy-start(f32[1024]{0:T(1024)} %param.34) | copy-start | bytes 12292
  194.4 18.8 %copy-start.8 = (f32[1024]{0:T(1024)S(1)}, f32[1024]{0:T(1024)}, u32[]{:S(2)}) copy-start(f32[1024]{0:T(1024)} %param.30) | copy-start | bytes 12292
  204.4 49.0 %all-gather.5.cloned.1.call-start = ((), (), s32[]{:S(2)}) async-start(), calls=%async_computation.3 | async-start | bytes 1114112 | tf_op jit(solution)/shard_map/all_gather | solution.py:204
Sparse Core Ops, SparseCore 0:
  9.5 40.7 all-gather.2
  204.5 8.6 reduce-scatter.1
  215.4 37.9 all-gather.4
where the time goes:
time: 263 us; the launch traced here: 262 us
  blocking collectives  118 us (45%)
  waiting for transfers between devices  61.9 us (24%)
  matrix products  33 us (13%)
  local copies, waits for them, and re-layouts  25.6 us (10%)
  between operations  16 us (6%)
  other arithmetic  7.06 us (3%)
    psum x1, blocking collectives, local(): long_queries = lax.psum(long_part, 'seq')  58.4 us
    all_gather x3, blocking collectives, merged(): everything = jax.tree.map(lambda part: lax.all_gather(part, axis), array)  54.8 us
    all_gather x1, waiting for transfers between devices, local(): lax.all_gather(finished, 'seq', axis=0, tiled=True)  38.6 us
    unnamed x25, local copies, waits for them, and re-layouts  17.2 us
    all_gather x1, waiting for transfers between devices, local(): shard_rows = lax.all_gather(tokens, 'seq', axis=0, tiled=True)  13.8 us
    dot_general x1, matrix products, local(): jnp.dot(hidden_units, w_down, preferred_element_type=jnp.float32)  9.99 us
    reduce_scatter x1, waiting for transfers between devices, local(): lax.psum_scatter(partial_sum.astype(jnp.bfloat16), 'head', scatter_dimens...  8.76 us
    dot_general x1, matrix products, local(): jnp.dot(normed_attn, w_qkv.reshape(w_qkv.shape[0], 3 * part_width), prefe...  8.47 us
  transfers between devices with their start and end apart: 3, of which 3 were waited for; matrix products, arithmetic and copies ran while one was open for 10% of the time, Pallas kernels for 0%

commit v1 on v0

--- a/solution.py
+++ b/solution.py
@@ -132,7 +132,8 @@
     long_part = jnp.sum(
         jnp.where(long_hits[:, :, None, None], queries.astype(jnp.float32)[:, None], 0.0), axis=0
     )
-    long_queries = lax.psum(long_part, "seq")
+    shards = lax.all_gather(long_part, "seq")
+    long_queries = jnp.sum(shards, axis=0)
     short_max = keys_short.shape[1]
     short_usable = (jnp.arange(short_max, dtype=jnp.int32)[None, :] < my_lengths[:, None]) & (
         my_lengths <= short_max

time: 263 us -> 225 us (0.86)
  blocking collectives: 118 us -> 79.6 us
    psum x1 -> x0, blocking collectives: 58.4 us -> none  [local(): long_queries = lax.psum(long_part, 'seq')]
    all_gather x0 -> x1, blocking collectives: none -> 20 us  [local(): shards = lax.all_gather(long_part, 'seq')]
  transfers between devices with their start and end apart: 3 -> 3, of which waited for: 3 -> 3; matrix products, arithmetic and copies ran while one was open for 10% -> 12% of each run, Pallas kernels for 0% -> 0%
where the time goes in v1:
time: 225 us; the launch traced here: 224 us
  blocking collectives  79.6 us (35%)
  waiting for transfers between devices  61.9 us (28%)
  matrix products  33 us (15%)
  local copies, waits for them, and re-layouts  25.6 us (11%)
  between operations  16 us (7%)
  other arithmetic  7.15 us (3%)
    all_gather x3, blocking collectives, merged(): everything = jax.tree.map(lambda part: lax.all_gather(part, axis), array)  54.7 us
    all_gather x1, waiting for transfers between devices, local(): lax.all_gather(finished, 'seq', axis=0, tiled=True)  38.6 us
    all_gather x1, blocking collectives, local(): shards = lax.all_gather(long_part, 'seq')  20 us
    unnamed x25, local copies, waits for them, and re-layouts  17.2 us
    all_gather x1, waiting for transfers between devices, local(): shard_rows = lax.all_gather(tokens, 'seq', axis=0, tiled=True)  13.8 us
    dot_general x1, matrix products, local(): jnp.dot(hidden_units, w_down, preferred_element_type=jnp.float32)  9.99 us
    reduce_scatter x1, waiting for transfers between devices, local(): lax.psum_scatter(partial_sum.astype(jnp.bfloat16), 'head', scatter_dimens...  8.73 us
    dot_general x1, matrix products, local(): jnp.dot(normed_attn, w_qkv.reshape(w_qkv.shape[0], 3 * part_width), prefe...  8.47 us
  transfers between devices with their start and end apart: 3, of which 3 were waited for; matrix products, arithmetic and copies ran while one was open for 12% of the time, Pallas kernels for 0%

profile of v1, /device:TPU:0, one launch (start us, length us, event | category | flops | bytes accessed | tf_op | source)
XLA Modules:
  0.0 223.7 jit_solution(15313449590345611683)
XLA Ops:
  6.5 0.7 all-gather.4.cloned.1.call-update
  7.3 1.2 dynamic_slice.37
  11.2 17.0 %copy.30 = bf16[2048,3,1024]{0,2,1:T(8,128)(2,1)} copy(bf16[2048,3,1024]{2,0,1:T(8,128)(2,1)} %param.27) | data formatting | bytes 25165824 | tf_op args[5]
  28.5 6.5 %copy.47 = bf16[2048,1024]{0,1:T(8,128)(2,1)} copy(bf16[2048,1024]{1,0:T(8,128)(2,1)} %param.37) | data formatting | bytes 8388608 | tf_op jit(solution)/shard_map/reshape.2
  35.0 0.6 select_reduce_fusion.6
  36.5 13.8 %all-gather.4.cloned.1.call-done = bf16[512,1024]{1,0:T(8,128)(2,1)} async-done(((bf16[32,1024]{1,0:T(8,128)(2,1)}), bf16[512,1024]{1,0:T(8,128)(2,1)}) %all-gather.4.cloned.1.call-update) | async-done | bytes 1048592 | tf_op jit(solution)/shard_map/all_gather | solution.py:104
  50.3 1.5 convolution_convert_fusion.1
  51.8 4.9 %all_gather.28 = bf16[32,2048]{1,0:T(8,128)(2,1)S(1)} all-gather(bf16[32,1024]{1,0:T(8,128)(2,1)S(1)} %convolution_convert_fusion.1), channel_id=1, replica_groups=mesh['seq'=16,'head'=2] {'head'}, dimensions={1}, use_global_device_ids=true | all-gather | bytes 196608 | tf_op jit(solution)/shard_map/all_gather | solution.py:110
  57.2 8.5 %fusion.15 = f32[32,3,1024]{2,0,1:T(8,128)S(1)} fusion(bf16[2048,3,1024]{0,2,1:T(8,128)(2,1)} %copy.30, f32[3,1024]{1,0:T(4,128)S(1)} %copy-done.1, bf16[32,2048]{1,0:T(8,128)(2,1)S(1)} %all_gather.28, f32[2048]{0:T(1024)S(1)} %copy-done.5, f32[2048]{0:T(1024)S(1)} %copy-done.6, f32[32]{0:T(128)S(1)} %add_rsqrt_fusion, f32[32]{0:T(128)S(1)} %broadcast_multiply_fusion), kind=kOutput, calls=%fused_computation.22 | convolution fusion | flops 403144704 | bytes 13136128 | tf_op jit(solution)/shard_map/dot_general | solution.py:114
  66.6 3.4 %fusion.11 = f32[32,4,1,64]{3,2,1,0:T(1,128)S(1)} fusion(bf16[32,8,4,8,256]{4,3,2,1,0:T(8,128)(2,1)} %bitcast.120, bf16[32,4,256,1]{2,1,0,3:T(4,128)(2,1)S(1)} %bitcast.117), kind=kOutput, calls=%fused_computation.16 | convolution fusion | flops 4194304 | bytes 4292608 | tf_op jit(solution)/shard_map/rhc,rthc->rht/dot_general | solution.py:49
  70.4 20.0 %all-gather = f32[64,4,256]{2,1,0:T(4,128)S(1)} all-gather(f32[4,4,256]{2,1,0:T(4,128)S(1)} %select_reduce_fusion.1), channel_id=2, replica_groups=mesh['seq'=16,'head'=2] {'seq'}, dimensions={0}, use_global_device_ids=true | all-gather | bytes 278528 | tf_op jit(solution)/shard_map/all_gather | solution.py:135
  90.6 3.0 %fusion.108 = f32[4,1,2048]{2,1,0:T(1,128)S(1)} fusion(bf16[2048,4,256]{0,2,1:T(8,128)(2,1)} %bitcast.113, bf16[4,256,1]{1,0,2:T(4,128)(2,1)S(1)} %bitcast.118), kind=kOutput, calls=%fused_computation.149 | convolution fusion | flops 4194304 | bytes 4229120 | tf_op jit(solution)/shard_map/rhc,rthc->rht/dot_general | solution.py:49
  93.9 0.7 fusion.5
  94.7 18.1 %all_gather.33 = f32[16,4,4,256]{3,2,1,0:T(4,128)S(1)} all-gather(f32[1,4,4,256]{3,2,1,0:T(4,128)S(1)} %broadcast_select_fusion), channel_id=1, replica_groups=mesh['seq'=16,'head'=2] {'seq'}, dimensions={0}, use_global_device_ids=true | all-gather | bytes 278528 | tf_op jit(solution)/shard_map/all_gather | solution.py:14
  112.9 18.8 %all_gather.32 = f32[16,4,4]{2,1,0:T(4,128)S(1)} all-gather(f32[1,4,4]{2,1,0:T(4,128)S(1)} %get-tuple-element.228), channel_id=1, replica_groups=mesh['seq'=16,'head'=2] {'seq'}, dimensions={0}, use_global_device_ids=true | all-gather | bytes 1088 | tf_op jit(solution)/shard_map/all_gather | solution.py:14
  131.7 17.7 %all_gather.31 = f32[16,4,4]{2,1,0:T(4,128)S(1)} all-gather(f32[1,4,4]{2,1,0:T(4,128)S(1)} %get-tuple-element.229), channel_id=1, replica_groups=mesh['seq'=16,'head'=2] {'seq'}, dimensions={0}, use_global_device_ids=true | all-gather | bytes 1088 | tf_op jit(solution)/shard_map/all_gather | solution.py:14
  149.4 2.0 while.19
  151.7 3.0 %fusion.8 = f32[32,4,1,256]{3,2,1,0:T(1,128)S(1)} fusion(bf16[32,8,4,8,256]{4,3,2,1,0:T(8,128)(2,1)} %bitcast.114, bf16[32,4,64,1]{2,0,1,3:T(8,128)(2,1)S(1)} %get-tuple-element.218), kind=kOutput, calls=%fused_computation.13 | convolution fusion | flops 4194304 | bytes 4341760 | tf_op jit(solution)/shard_map/rht,rthc->rhc/dot_general | solution.py:56
  155.1 0.8 fusion.143
  156.0 10.0 %fusion.14 = bf16[32,2048]{1,0:T(8,128)(2,1)} fusion(f32[32,2048]{1,0:T(8,128)S(1)} %fusion.143, bf16[2048,2048]{1,0:T(8,128)(2,1)} %param.33, bf16[2048,2048]{1,0:T(8,128)(2,1)} %param.31, bf16[32,2048]{1,0:T(8,128)(2,1)S(1)} %all_gather.28, f32[2048]{0:T(1024)S(1)} %copy-done.2, f32[2048]{0:T(1024)S(1)} %copy-done.3, f32[2048]{0:T(1024)S(1)} %copy-done.4, ...), kind=kOutput, calls=%fused_computation.21 | convolution fusion | flops 541720576 | bytes 17326336 | tf_op jit(solution)/shard_map/dot_general | solution.py:194
  166.1 8.7 %reduce-scatter.2.cloned.1.call-done = bf16[32,1024]{1,0:T(8,128)(2,1)} async-done(((bf16[32,2048]{1,0:T(8,128)(2,1)}), bf16[32,1024]{1,0:T(8,128)(2,1)}) %reduce-scatter.2.cloned.1.call-update) | async-done | bytes 65552 | tf_op jit(solution)/shard_map/reduce_scatter | solution.py:197
  174.8 1.5 add_convert_fusion
  176.3 38.6 %all-gather.6.cloned.1.call-done = bf16[512,1024]{1,0:T(8,128)(2,1)} async-done(((bf16[32,1024]{1,0:T(8,128)(2,1)}), bf16[512,1024]{1,0:T(8,128)(2,1)}) %all-gather.6.cloned.1.call-update) | async-done | bytes 1048592 | tf_op jit(solution)/shard_map/all_gather | solution.py:205
  214.9 2.2 convolution_convert_fusion
  (103 shorter events, 6.0 us)
Async XLA Ops:
  6.5 43.8 %all-gather.4.cloned.1.call-start = ((), (), s32[]{:S(2)}) async-start(), calls=%async_computation.1 | async-start | bytes 1114112 | tf_op jit(solution)/shard_map/all_gather | solution.py:104
  7.3 167.5 %reduce-scatter.2.cloned.1.call-start = ((), (), s32[]{:S(2)}) async-start(), calls=%async_computation.2 | async-start | bytes 196608 | tf_op jit(solution)/shard_map/reduce_scatter | solution.py:197
  11.2 17.0 %copy-start.9 = (s32[512]{0:T(512)S(1)}, s32[512]{0:T(512)}, u32[]{:S(2)}) copy-start(s32[512]{0:T(512)} %param.40) | copy-start | bytes 6148
  11.2 17.1 %copy-start.10 = (s32[512]{0:T(512)S(1)}, s32[512]{0:T(512)}, u32[]{:S(2)}) copy-start(s32[512]{0:T(512)} %param.39) | copy-start | bytes 6148
  28.4 28.7 %copy-start.1 = (f32[3,1024]{1,0:T(4,128)S(1)}, f32[3,1024]{1,0:T(4,128)}, u32[]{:S(2)}) copy-start(f32[3,1024]{1,0:T(4,128)} %param.28) | copy-start | bytes 36868
  28.4 28.7 %copy-start.5 = (f32[2048]{0:T(1024)S(1)}, f32[2048]{0:T(1024)}, u32[]{:S(2)}) copy-start(f32[2048]{0:T(1024)} %param.24) | copy-start | bytes 24580
  28.5 28.7 %copy-start.6 = (f32[2048]{0:T(1024)S(1)}, f32[2048]{0:T(1024)}, u32[]{:S(2)}) copy-start(f32[2048]{0:T(1024)} %param.23) | copy-start | bytes 24580
  90.5 3.4 %copy-start.11 = (bf16[2048,1024]{1,0:T(8,128)(2,1)S(1)}, bf16[2048,1024]{1,0:T(8,128)(2,1)}, u32[]{:S(2)}) copy-start(bf16[2048,1024]{1,0:T(8,128)(2,1)} %param.38) | copy-start | bytes 12582916
  151.7 3.5 %copy-start = (bf16[1024,2048]{1,0:T(8,128)(2,1)S(1)}, bf16[1024,2048]{1,0:T(8,128)(2,1)}, u32[]{:S(2)}) copy-start(bf16[1024,2048]{1,0:T(8,128)(2,1)} %param.29) | copy-start | bytes 12582916
  151.7 4.3 %copy-start.2 = (f32[2048]{0:T(1024)S(1)}, f32[2048]{0:T(1024)}, u32[]{:S(2)}) copy-start(f32[2048]{0:T(1024)} %param.32) | copy-start | bytes 24580
  151.7 4.3 %copy-start.3 = (f32[2048]{0:T(1024)S(1)}, f32[2048]{0:T(1024)}, u32[]{:S(2)}) copy-start(f32[2048]{0:T(1024)} %param.26) | copy-start | bytes 24580
  151.7 4.3 %copy-start.4 = (f32[2048]{0:T(1024)S(1)}, f32[2048]{0:T(1024)}, u32[]{:S(2)}) copy-start(f32[2048]{0:T(1024)} %param.25) | copy-start | bytes 24580
  156.0 18.8 %copy-start.7 = (f32[1024]{0:T(1024)S(1)}, f32[1024]{0:T(1024)}, u32[]{:S(2)}) copy-start(f32[1024]{0:T(1024)} %param.34) | copy-start | bytes 12292
  156.0 18.8 %copy-start.8 = (f32[1024]{0:T(1024)S(1)}, f32[1024]{0:T(1024)}, u32[]{:S(2)}) copy-start(f32[1024]{0:T(1024)} %param.30) | copy-start | bytes 12292
  166.0 48.9 %all-gather.6.cloned.1.call-start = ((), (), s32[]{:S(2)}) async-start(), calls=%async_computation.3 | async-start | bytes 1114112 | tf_op jit(solution)/shard_map/all_gather | solution.py:205
Sparse Core Ops, SparseCore 0:
  9.5 40.7 all-gather.3
  166.1 8.6 reduce-scatter.1
  177.0 37.9 all-gather.5
